TPU v7x, 32 devices: a whole 2x2x4 slice. The times are simulated.
32 devices in a mesh: groups: 2 (over x), blk: 4 (over y, core), width: 4 (over z).
Axes of the slice: x: 2, y: 2, z: 4, core: 2. Of those that a mesh axis runs over, the one named last changes fastest.
Arguments:
- activations: float32 [8192, 8192], P(('groups', 'blk'), 'width'), parts along dimension 0, may hold values from -6 to 6
- query_grads: float32 [16, 8192, 128], P(('groups', 'blk'), 'width'), parts along dimension 0, may hold values from -0.0625 to 0.0625
- outgrad_proj: float32 [8192, 128], P(('groups', 'blk', 'width')), parts along dimension 0, may hold values from -0.6 to 0.6
- doc_ids: int32 [8192], P(('groups', 'blk', 'width')), parts along dimension 0, may hold values from 0 to 15, never falling along the last dimension, each value on 1 to 512 neighbouring positions
Outputs:
- token_scores: float32 [8192, 8], P(('groups', 'blk', 'width')), parts along dimension 0
- doc_scores: float32 [32, 8], P('groups'), parts along dimension 0
There are 2 independent parts, one for each index of `groups`. A program takes and returns all parts, laid end to end along the dimension named above; each array names one. Nothing has to cross between parts.
Inputs may be any that keep to these rules, and one draw needn't show every extreme that they name: `doc_ids`: never falls along the tokens; every document 0 to 15 holds 1 to 512 tokens, one exactly 512.
All inputs are finite; a program needn't handle non-finite values.
Results may differ from a plain program's by a relative error of at most 0.000078.
Values sent between devices are 32-bit elements; how exact they have to be, the bound alone decides.
No kernel may reach another device: no remote copies, remote signals or barrier semaphores. Data moves between devices by JAX's collectives and lax.ppermute only.
A program may use at most 128 MiB of HBM per device.

v0:
```python
import jax
import jax.numpy as jnp
from jax import lax
from jax.sharding import PartitionSpec as P

DOC_BLK = 4


def per_device(activations, query_grads, outgrad_proj, doc_ids):
    projected = jnp.einsum(
        "td,qdr->tqr",
        activations,
        lax.all_gather(query_grads, "blk", axis=0, tiled=True),
        precision=lax.Precision.HIGHEST,
        preferred_element_type=jnp.float32,
    )
    owned_parts = lax.psum_scatter(projected, "width", scatter_dimension=0, tiled=True)
    token_scores = jnp.sum(owned_parts * outgrad_proj[:, None, :], axis=2)
    doc_total = DOC_BLK * lax.axis_size("blk")
    doc_range = jnp.arange(doc_total, dtype=jnp.int32)
    onehot = (doc_ids[:, None] == doc_range[None, :]).astype(jnp.float32)
    doc_sums = jnp.einsum(
        "tn,tq->nq",
        onehot,
        token_scores,
        precision=lax.Precision.HIGHEST,
        preferred_element_type=jnp.float32,
    )
    doc_counts = jnp.sum(onehot, axis=0)
    doc_sums, doc_counts = lax.psum((doc_sums, doc_counts), ("blk", "width"))
    doc_scores = doc_sums / jnp.sqrt(doc_counts)[:, None]
    return (token_scores, doc_scores)


def solution(mesh):
    return jax.shard_map(
        per_device,
        mesh=mesh,
        in_specs=(
            P(("groups", "blk"), "width"),
            P(("groups", "blk"), "width", None),
            P(("groups", "blk", "width"), None),
            P(("groups", "blk", "width")),
        ),
        out_specs=(P(("groups", "blk", "width"), None), P("groups", None)),
        check_vma=False,
    )
```

profile of v0, /device:TPU:0, one launch (start us, length us, event | category | flops | bytes accessed | tf_op | source)
XLA Modules:
  0.0 222.9 jit_solution(11770008080408502427)
XLA Ops:
  7.2 0.0 all-gather.2.cloned.1.call-start
  7.2 0.7 all-gather.2.cloned.1.call-update
  7.9 0.0 copy-start.2
  7.9 0.0 copy-start
  7.9 0.0 reduce-scatter.2.cloned.1.call-start
  8.0 62.6 %all-gather.2.cloned.1.call-done = f32[8,2048,128]{2,1,0:T(8,128)} async-done(((f32[2,2048,128]{2,1,0:T(8,128)}), f32[8,2048,128]{2,1,0:T(8,128)}) %all-gather.2.cloned.1.call-update) | async-done | bytes 8388624 | tf_op jit(solution)/shard_map/all_gather | solution.py:13
  70.6 32.7 %fusion = f32[1024,8,128]{2,0,1:T(8,128)} fusion(f32[8,2048,128]{2,1,0:T(8,128)} %all-gather.2.cloned.1.call-done, f32[1024,2048]{1,0:T(8,128)} %param.4), kind=kOutput, calls=%fused_computation | convolution fusion | flops 25769803776 | bytes 20971520 | tf_op jit(solution)/shard_map/td,qdr->tqr/dot_general | solution.py:10
  103.3 0.0 reduce-scatter.2.cloned.1.call-update
  103.3 0.0 copy-done.2
  103.3 0.1 convert_reduce_fusion
  103.4 76.8 %reduce-scatter.2.cloned.1.call-done = f32[256,8,128]{2,0,1:T(8,128)} async-done(((f32[1024,8,128]{2,0,1:T(8,128)}), f32[256,8,128]{2,0,1:T(8,128)}) %reduce-scatter.2.cloned.1.call-update) | async-done | bytes 1048592 | tf_op jit(solution)/shard_map/reduce_scatter | solution.py:17
  180.2 0.0 copy-done
  180.2 1.6 multiply_reduce_fusion
  181.8 0.0 copy-start.1
  181.8 0.1 fusion.2
  181.9 33.5 %all-reduce = (f32[16,8]{0,1:T(8,128)S(1)}, f32[16]{0:T(128)S(1)}) all-reduce(f32[16,8]{0,1:T(8,128)S(1)} %fusion.2, f32[16]{0:T(128)S(1)} %convert_reduce_fusion), channel_id=1, replica_groups=mesh['groups'=2,'blk'=4,'width'=4] {'blk','width'}, use_global_device_ids=true, to_apply=%region_2.0 | all-reduce | flops 144 | bytes 1152 | tf_op jit(solution)/shard_map/psum | solution.py:30
  215.5 0.6 broadcast_divide_fusion
  216.1 0.0 copy-done.1
  (1 shorter events, 0.0 us)
Async XLA Ops:
  7.2 63.4 %all-gather.2.cloned.1.call-start = ((), (), s32[]{:S(2)}) async-start(), calls=%async_computation.1 | async-start | bytes 10485760 | tf_op jit(solution)/shard_map/all_gather | solution.py:13
  7.9 95.4 %copy-start.2 = (s32[256]{0:T(256)S(1)}, s32[256]{0:T(256)}, u32[]{:S(2)}) copy-start(s32[256]{0:T(256)} %param.7) | copy-start | bytes 3076
  7.9 172.3 %copy-start = (f32[256,128]{1,0:T(8,128)S(1)}, f32[256,128]{1,0:T(8,128)}, u32[]{:S(2)}) copy-start(f32[256,128]{1,0:T(8,128)} %param.6) | copy-start | bytes 393220
  7.9 172.3 %reduce-scatter.2.cloned.1.call-start = ((), (), s32[]{:S(2)}) async-start(), calls=%async_computation.2 | async-start | bytes 5242880 | tf_op jit(solution)/shard_map/reduce_scatter | solution.py:17
  181.8 34.3 %copy-start.1 = (f32[256,8]{0,1:T(8,128)}, f32[256,8]{0,1:T(8,128)S(1)}, u32[]{:S(2)}) copy-start(f32[256,8]{0,1:T(8,128)S(1)} %multiply_reduce_fusion) | copy-start | bytes 24580
Sparse Core Ops, SparseCore 0:
  9.6 60.9 all-gather.1
  103.4 76.7 reduce-scatter.1
where the time goes:
time: 223 us
  waiting for transfers between devices  140 us (63%)
  blocking collectives  33.5 us (15%)
  matrix products  32.8 us (15%)
  between operations  14.1 us (6%)
  other arithmetic  2.29 us (1%)
    reduce_scatter x1, waiting for transfers between devices, per_device(): lax.psum_scatter(projected, 'width', scatter_dimension=0, tiled=True)  76.8 us
    all_gather x1, waiting for transfers between devices, per_device(): lax.all_gather(query_grads, 'blk', axis=0, tiled=True)  62.6 us
    psum x1, blocking collectives, per_device(): doc_sums, doc_counts = lax.psum((doc_sums, doc_counts), ('blk', 'width'))  33.5 us
    dot_general x1, matrix products, per_device(): jnp.einsum('td,qdr->tqr', activations, lax.all_gather(query_grads, 'blk',...  32.7 us
  transfers between devices with their start and end apart: 2, of which 2 were waited for; matrix products, arithmetic and copies ran while one was open for 0% of the time, Pallas kernels for 0%

commit v1 on v0

--- a/solution.py
+++ b/solution.py
@@ -6,13 +6,34 @@
 DOC_BLK = 4
 
 
+def ring_apply(x, axis, dim, make, out_dim):
+    ways, here, step = (lax.axis_size(axis), lax.axis_index(axis), x.shape[dim])
+    results = []
+    for far in range(ways):
+        arriving = (
+            lax.ppermute(x, axis, [(d, (d + 1) % ways) for d in range(ways)])
+            if far + 1 < ways
+            else x
+        )
+        results.append(make(x, (here - far) % ways * step))
+        x = arriving
+    line = jnp.concatenate(results[::-1], axis=out_dim)
+    return jnp.roll(line, (here + 1) * results[0].shape[out_dim], axis=out_dim)
+
+
 def per_device(activations, query_grads, outgrad_proj, doc_ids):
-    projected = jnp.einsum(
-        "td,qdr->tqr",
-        activations,
-        lax.all_gather(query_grads, "blk", axis=0, tiled=True),
-        precision=lax.Precision.HIGHEST,
-        preferred_element_type=jnp.float32,
+    projected = ring_apply(
+        query_grads,
+        "blk",
+        0,
+        lambda own_block, start: jnp.einsum(
+            "td,qdr->tqr",
+            activations,
+            own_block,
+            precision=lax.Precision.HIGHEST,
+            preferred_element_type=jnp.float32,
+        ),
+        1,
     )
     owned_parts = lax.psum_scatter(projected, "width", scatter_dimension=0, tiled=True)
     token_scores = jnp.sum(owned_parts * outgrad_proj[:, None, :], axis=2)

time: 223 us -> 241 us (1.081)
  waiting for transfers between devices: 140 us -> 156 us
  local copies, waits for them, and re-layouts: 0.02 us -> 2.53 us
    ppermute x0 -> x3, waiting for transfers between devices: none -> 77.2 us  [ring_apply(): lax.ppermute(x, axis, [(d, (d + 1) % ways) for d in range(ways)])]
    all_gather x1 -> x0, waiting for transfers between devices: 62.6 us -> none  [per_device(): lax.all_gather(query_grads, 'blk', axis=0, tiled=True)]
    dot_general x1 -> x4, matrix products: 32.7 us -> 31.4 us  [per_device(): jnp.einsum('td,qdr->tqr', activations, own_block, precision=lax.Precision...]
  transfers between devices with their start and end apart: 2 -> 4, of which waited for: 2 -> 4; matrix products, arithmetic and copies ran while one was open for 0% -> 0% of each run, Pallas kernels for 0% -> 0%
where the time goes in v1:
time: 241 us
  waiting for transfers between devices  156 us (65%)
  blocking collectives  33.5 us (14%)
  matrix products  31.5 us (13%)
  between operations  14.2 us (6%)
  local copies, waits for them, and re-layouts  2.53 us (1%)
    reduce_scatter x1, waiting for transfers between devices, per_device(): lax.psum_scatter(projected, 'width', scatter_dimension=0, tiled=True)  78.8 us
    ppermute x3, waiting for transfers between devices, ring_apply(): lax.ppermute(x, axis, [(d, (d + 1) % ways) for d in range(ways)])  77.2 us
    psum x1, blocking collectives, per_device(): doc_sums, doc_counts = lax.psum((doc_sums, doc_counts), ('blk', 'width'))  33.5 us
    dot_general x4, matrix products, per_device(): jnp.einsum('td,qdr->tqr', activations, own_block, precision=lax.Precision...  31.4 us
  transfers between devices with their start and end apart: 4, of which 4 were waited for; matrix products, arithmetic and copies ran while one was open for 0% of the time, Pallas kernels for 0%

profile of v1, /device:TPU:0, one launch (start us, length us, event | category | flops | bytes accessed | tf_op | source)
XLA Modules:
  0.0 240.6 jit_solution(2954230430260356823)
XLA Ops:
  7.2 0.0 reduce-scatter.2.cloned.1.call-start
  7.2 0.5 collective-permute-start
  7.7 25.9 %collective-permute-done = f32[2,2048,128]{2,1,0:T(8,128)S(1)} collective-permute-done((f32[2,2048,128]{2,1,0:T(8,128)}, f32[2,2048,128]{2,1,0:T(8,128)S(1)}, u32[]{:S(2)}, u32[]{:S(2)}) %collective-permute-start) | collective-permute-done | bytes 2097184 | tf_op jit(solution)/shard_map/ppermute | solution.py:14
  33.6 0.0 collective-permute-start.1
  33.6 25.5 %collective-permute-done.1 = f32[2,2048,128]{2,1,0:T(8,128)} collective-permute-done((f32[2,2048,128]{2,1,0:T(8,128)S(1)}, f32[2,2048,128]{2,1,0:T(8,128)}, u32[]{:S(2)}, u32[]{:S(2)}) %collective-permute-start.1) | collective-permute-done | bytes 2097184 | tf_op jit(solution)/shard_map/ppermute | solution.py:14
  59.2 0.0 collective-permute-start.2
  59.2 0.0 copy-start
  59.2 25.8 %collective-permute-done.2 = f32[2,2048,128]{2,1,0:T(8,128)} collective-permute-done((f32[2,2048,128]{2,1,0:T(8,128)}, f32[2,2048,128]{2,1,0:T(8,128)}, u32[]{:S(2)}, u32[]{:S(2)}) %collective-permute-start.2) | collective-permute-done | bytes 2097184 | tf_op jit(solution)/shard_map/ppermute | solution.py:14
  84.9 9.6 %constant_dynamic-update-slice_fusion.7 = (f32[1024,16,128]{2,0,1:T(8,128)S(1)}, f32[1024,2,128]{2,0,1:T(8,128)S(1)}) fusion(f32[2,2048,128]{2,1,0:T(8,128)} %collective-permute-done.2, f32[1024,2048]{1,0:T(8,128)} %param.4), kind=kOutput, calls=%fused_computation.16 | convolution fusion | flops 6442450944 | bytes 12582912 | tf_op jit(solution)/shard_map/td,qdr->tqr/dot_general | solution.py:29
  94.5 0.0 copy-done
  94.6 8.2 %constant_dynamic-update-slice_fusion.6 = (f32[1024,16,128]{2,0,1:T(8,128)S(1)}, f32[1024,2,128]{2,0,1:T(8,128)S(1)}) fusion(f32[1024,16,128]{2,0,1:T(8,128)S(1)} %get-tuple-element.4, f32[2,2048,128]{2,1,0:T(8,128)} %collective-permute-done.1, f32[1024,2048]{1,0:T(8,128)S(1)} %copy-done), kind=kOutput, calls=%fused_computation.15 | convolution fusion | flops 6442450944 | bytes 12582912 | tf_op jit(solution)/shard_map/td,qdr->tqr/dot_general | solution.py:29
  102.8 0.0 copy-start.1
  102.8 6.9 %constant_dynamic-update-slice_fusion.5 = (f32[1024,16,128]{2,0,1:T(8,128)S(1)}, f32[1024,2,128]{2,0,1:T(8,128)S(1)}) fusion(f32[1024,16,128]{2,0,1:T(8,128)S(1)} %get-tuple-element.6, f32[2,2048,128]{2,1,0:T(8,128)S(1)} %collective-permute-done, f32[1024,2048]{1,0:T(8,128)S(1)} %copy-done), kind=kOutput, calls=%fused_computation.14 | convolution fusion | flops 6442450944 | bytes 12582912 | tf_op jit(solution)/shard_map/td,qdr->tqr/dot_general | solution.py:29
  109.7 0.0 copy-done.1
  109.7 6.7 %constant_dynamic-update-slice_fusion.4 = (f32[1024,16,128]{2,0,1:T(8,128)S(1)}, f32[1024,2,128]{2,0,1:T(8,128)S(1)}) fusion(f32[1024,16,128]{2,0,1:T(8,128)S(1)} %get-tuple-element.8, f32[2,2048,128]{2,1,0:T(8,128)S(1)} %copy-done.1, f32[1024,2048]{1,0:T(8,128)S(1)} %copy-done), kind=kOutput, calls=%fused_computation.13 | convolution fusion | flops 6442450944 | bytes 12582912 | tf_op jit(solution)/shard_map/td,qdr->tqr/dot_general | solution.py:29
  116.4 0.1 constant_dynamic-update-slice_fusion.3
  116.5 0.1 constant_dynamic-update-slice_fusion.2
  116.6 0.0 copy-start.4
  116.6 0.0 copy-start.2
  116.6 0.1 constant_dynamic-update-slice_fusion.1
  116.7 0.1 constant_dynamic-update-slice_fusion
  116.7 2.2 constant_dynamic-slice_fusion
  119.0 0.0 reduce-scatter.2.cloned.1.call-update
  119.0 0.0 copy-done.4
  119.0 0.1 convert_reduce_fusion
  119.1 78.8 %reduce-scatter.2.cloned.1.call-done = f32[256,8,128]{2,0,1:T(8,128)} async-done(((f32[1024,8,128]{2,0,1:T(8,128)}), f32[256,8,128]{2,0,1:T(8,128)}) %reduce-scatter.2.cloned.1.call-update) | async-done | bytes 1048592 | tf_op jit(solution)/shard_map/reduce_scatter | solution.py:38
  197.9 0.0 copy-done.2
  197.9 1.6 multiply_reduce_fusion
  199.5 0.0 copy-start.3
  199.5 0.1 fusion.8
  199.7 33.5 %all-reduce = (f32[16,8]{0,1:T(8,128)S(1)}, f32[16]{0:T(128)S(1)}) all-reduce(f32[16,8]{0,1:T(8,128)S(1)} %fusion.8, f32[16]{0:T(128)S(1)} %convert_reduce_fusion), channel_id=1, replica_groups=mesh['groups'=2,'blk'=4,'width'=4] {'blk','width'}, use_global_device_ids=true, to_apply=%region_2.3 | all-reduce | flops 144 | bytes 1152 | tf_op jit(solution)/shard_map/psum | solution.py:51
  233.2 0.6 broadcast_divide_fusion
  233.8 0.0 copy-done.3
  (1 shorter events, 0.0 us)
Async XLA Ops:
  7.2 190.8 %reduce-scatter.2.cloned.1.call-start = ((), (), s32[]{:S(2)}) async-start(), calls=%async_computation.1 | async-start | bytes 5242880 | tf_op jit(solution)/shard_map/reduce_scatter | solution.py:38
  7.2 26.4 %collective-permute-start = (f32[2,2048,128]{2,1,0:T(8,128)}, f32[2,2048,128]{2,1,0:T(8,128)S(1)}, u32[]{:S(2)}, u32[]{:S(2)}) collective-permute-start(f32[2,2048,128]{2,1,0:T(8,128)} %param.5), channel_id=1, source_target_pairs={{0,4},{4,8},{8,12},{12,0},{1,5},{5,9},{9,13},{13,1},{2,6},{6,10},{... | collective-permute-start | bytes 6291464 | tf_op jit(solution)/shard_map/ppermute | solution.py:14
  33.6 25.6 %collective-permute-start.1 = (f32[2,2048,128]{2,1,0:T(8,128)S(1)}, f32[2,2048,128]{2,1,0:T(8,128)}, u32[]{:S(2)}, u32[]{:S(2)}) collective-permute-start(f32[2,2048,128]{2,1,0:T(8,128)S(1)} %collective-permute-done), channel_id=1, source_target_pairs={{0,4},{4,8},{8,12},{12,0},{1,5},{5,9},{9,13},{13,1},{2,6},{6,10},{... | collective-permute-start | bytes 6291464 | tf_op jit(solution)/shard_map/ppermute | solution.py:14
  59.2 25.8 %collective-permute-start.2 = (f32[2,2048,128]{2,1,0:T(8,128)}, f32[2,2048,128]{2,1,0:T(8,128)}, u32[]{:S(2)}, u32[]{:S(2)}) collective-permute-start(f32[2,2048,128]{2,1,0:T(8,128)} %collective-permute-done.1), channel_id=1, source_target_pairs={{0,4},{4,8},{8,12},{12,0},{1,5},{5,9},{9,13},{13,1},{2,6},{6,10},{... | collective-permute-start | bytes 6291464 | tf_op jit(solution)/shard_map/ppermute | solution.py:14
  59.2 35.4 %copy-start = (f32[1024,2048]{1,0:T(8,128)S(1)}, f32[1024,2048]{1,0:T(8,128)}, u32[]{:S(2)}) copy-start(f32[1024,2048]{1,0:T(8,128)} %param.4) | copy-start | bytes 25165828
  102.8 6.9 %copy-start.1 = (f32[2,2048,128]{2,1,0:T(8,128)S(1)}, f32[2,2048,128]{2,1,0:T(8,128)}, u32[]{:S(2)}) copy-start(f32[2,2048,128]{2,1,0:T(8,128)} %param.5) | copy-start | bytes 6291460
  116.6 2.4 %copy-start.4 = (s32[256]{0:T(256)S(1)}, s32[256]{0:T(256)}, u32[]{:S(2)}) copy-start(s32[256]{0:T(256)} %param.7) | copy-start | bytes 3076
  116.6 81.4 %copy-start.2 = (f32[256,128]{1,0:T(8,128)S(1)}, f32[256,128]{1,0:T(8,128)}, u32[]{:S(2)}) copy-start(f32[256,128]{1,0:T(8,128)} %param.6) | copy-start | bytes 393220
  199.5 34.3 %copy-start.3 = (f32[256,8]{0,1:T(8,128)}, f32[256,8]{0,1:T(8,128)S(1)}, u32[]{:S(2)}) copy-start(f32[256,8]{0,1:T(8,128)S(1)} %multiply_reduce_fusion) | copy-start | bytes 24580
Sparse Core Ops, SparseCore 0:
  119.1 78.7 reduce-scatter.1
